TPU v7x, 512 devices: a whole 4x4x16 slice. The times are simulated.
512 devices in a mesh: seq: 64 (over y_lo, z, core), tensor: 8 (over x, y_hi).
Axes of the slice: x: 4, y: 4 (y_hi: 2, y_lo: 2; y = y_hi * 2 + y_lo), z: 16, core: 2. Of those that a mesh axis runs over, the one named last changes fastest.
Arguments:
- trunk: bfloat16 [2, 4096, 1536], P(None, 'seq', 'tensor'), may hold values from -12 to 12
- w_out: bfloat16 [1536, 1536], P('tensor', 'seq'), may hold values from -1 to 1
- gain_coarse: float32 [1536], replicated, may hold values from 0.1 to 1.9
- w_conv1: bfloat16 [5, 1536, 1536], P(None, 'seq', 'tensor'), may hold values from -0.0625 to 0.0625
- w_up: bfloat16 [1536, 2, 768], P('seq', None, 'tensor'), may hold values from -0.15625 to 0.15625
- skip: bfloat16 [2, 8192, 768], P(None, 'seq', 'tensor'), may hold values from -12 to 12
- gain_fine: float32 [768], replicated, may hold values from 0.1 to 1.9
- w_conv2: bfloat16 [5, 768, 768], P(None, 'seq', 'tensor'), may hold values from -0.09375 to 0.09375
- cotangent: bfloat16 [2, 8192, 768], P(None, 'seq', 'tensor'), may hold values from -6 to 6
Outputs:
- decoded: bfloat16 [2, 8192, 768], P(None, 'seq', 'tensor')
- skip_grad: bfloat16 [2, 8192, 768], P(None, 'seq', 'tensor')
- trunk_grad: bfloat16 [2, 4096, 1536], P(None, 'seq', 'tensor')
All inputs are finite; a program needn't handle non-finite values.
Results may differ from a plain program's by a relative error of at most 0.02.
Values may be sent and summed in bfloat16 or wider, within the bound.
No kernel may reach another device: no remote copies, remote signals or barrier semaphores. Data moves between devices by JAX's collectives and lax.ppermute only.
A program may use at most 64 MiB of HBM per device.

v0:
```python
import jax
import jax.numpy as jnp
from jax import lax
from jax.sharding import PartitionSpec as P

C_COARSE = 1536
C_FINE = 768
EPS = 1e-06


def extended(shard, sides, width):
    for axis, dim in sides:
        size, length = (lax.axis_size(axis), shard.shape[dim])
        up = [(i, (i + 1) % size) for i in range(size - 1)]
        down = [(j, i) for i, j in up]
        last = lax.slice_in_dim(shard, length - width, length, axis=dim)
        leading = lax.slice_in_dim(shard, 0, width, axis=dim)
        before = lax.ppermute(last, axis, up)
        after = lax.ppermute(leading, axis, down)
        shard = jnp.concatenate([before, shard, after], axis=dim)
    return shard


def matmul(left, right):
    return lax.dot_general(
        left, right, (((left.ndim - 1,), (0,)), ((), ())), preferred_element_type=jnp.float32
    )


def matmul_back(left, right):
    return lax.dot_general(
        left,
        right,
        (((left.ndim - 1,), (right.ndim - 1,)), ((), ())),
        preferred_element_type=jnp.float32,
    )


def activate(field, gain):
    scaled = field * lax.rsqrt(jnp.mean(field * field, axis=-1, keepdims=True) + EPS)
    return jax.nn.gelu(scaled * gain)


def widen(field):
    return extended(field, (("seq", 1),), 2)


def spread(field):
    return lax.all_gather(field, "tensor", axis=2, tiled=True)


def conv_rows(total, wide, piece):
    length = wide.shape[1] - 4
    for k in range(5):
        total = total + matmul(wide[:, k : k + length], piece[k])
    return total


def conv_back(wide_grad, piece):
    length = wide_grad.shape[1] - 4
    total = jnp.zeros((wide_grad.shape[0], length, piece.shape[1]), jnp.float32)
    for k in range(5):
        total = total + matmul_back(wide_grad[:, 4 - k : 4 - k + length], piece[k])
    return total


def norm_back(partial_grad, field_full, gain, rank, part):
    field = field_full.astype(jnp.float32)
    start = rank * part
    whole = lax.psum(partial_grad.astype(jnp.bfloat16), "tensor").astype(jnp.float32)

    def apply(value):
        return activate(value, gain)

    _, pull = jax.vjp(apply, field)
    return lax.dynamic_slice_in_dim(pull(whole)[0], start, part, 2)


def per_device(trunk, w_out, gain_coarse, w_conv1, w_up, skip, gain_fine, w_conv2, cotangent):
    rank = lax.axis_index("tensor")
    part_coarse = C_COARSE // lax.axis_size("tensor")
    part_fine = C_FINE // lax.axis_size("tensor")
    seqs = trunk.shape[0]
    slab = trunk.shape[1]
    out_w, up_w, conv2_w = (
        lax.all_gather(w_out, "seq", axis=1, tiled=True),
        lax.all_gather(w_up, "seq", axis=0, tiled=True),
        lax.all_gather(w_conv2, "seq", axis=1, tiled=True),
    )
    partial_proj = matmul(trunk, out_w)
    projected = lax.psum_scatter(
        partial_proj.astype(jnp.bfloat16), "tensor", scatter_dimension=2, tiled=True
    )
    projected_full = lax.all_gather(projected, "tensor", axis=2, tiled=True)
    act_coarse = activate(projected_full.astype(jnp.float32), gain_coarse).astype(jnp.bfloat16)
    coarse_wide = widen(act_coarse)
    empty_coarse = jnp.zeros((seqs, slab, part_coarse), jnp.float32)
    mixed_coarse = conv_rows(
        empty_coarse, coarse_wide, lax.all_gather(w_conv1, "seq", axis=1, tiled=True)
    )
    lifted = (projected.astype(jnp.float32) + mixed_coarse).astype(jnp.bfloat16)
    lifted_full = spread(lifted)
    upper = matmul(lifted_full, up_w).reshape(seqs, 2 * slab, part_fine)
    merged = (upper + skip.astype(jnp.float32)).astype(jnp.bfloat16)
    merged_full = spread(merged)
    act_fine = activate(merged_full.astype(jnp.float32), gain_fine).astype(jnp.bfloat16)
    fine_wide = widen(act_fine)
    empty_fine = jnp.zeros((seqs, 2 * slab, part_fine), jnp.float32)
    mixed_fine = conv_rows(empty_fine, fine_wide, conv2_w)
    decoded = (merged.astype(jnp.float32) + mixed_fine).astype(jnp.bfloat16)
    cot_wide = widen(cotangent)
    back_fine = conv_back(cot_wide, conv2_w)
    skip_grad = (
        cotangent.astype(jnp.float32)
        + norm_back(back_fine, merged_full, gain_fine, rank, part_fine)
    ).astype(jnp.bfloat16)
    folded = skip_grad.reshape(seqs, slab, 2 * part_fine)
    up_partial = matmul_back(folded, up_w.reshape(up_w.shape[0], 2 * part_fine))
    lifted_grad = lax.psum_scatter(
        up_partial.astype(jnp.bfloat16), "tensor", scatter_dimension=2, tiled=True
    )
    grad_wide = widen(lifted_grad)
    back_coarse = conv_back(grad_wide, lax.all_gather(w_conv1, "seq", axis=1, tiled=True))
    projected_grad = (
        lifted_grad.astype(jnp.float32)
        + norm_back(back_coarse, projected_full, gain_coarse, rank, part_coarse)
    ).astype(jnp.bfloat16)
    grad_full = spread(projected_grad)
    trunk_grad = matmul_back(grad_full, out_w).astype(jnp.bfloat16)
    return (decoded, skip_grad, trunk_grad)


def solution(mesh):
    in_specs = (
        P(None, "seq", "tensor"),
        P("tensor", "seq"),
        P(),
        P(None, "seq", "tensor"),
        P("seq", None, "tensor"),
        P(None, "seq", "tensor"),
        P(),
        P(None, "seq", "tensor"),
        P(None, "seq", "tensor"),
    )
    out_specs = (P(None, "seq", "tensor"), P(None, "seq", "tensor"), P(None, "seq", "tensor"))
    return jax.shard_map(
        per_device, mesh=mesh, in_specs=in_specs, out_specs=out_specs, check_vma=False
    )
```

profile of v0, /device:TPU:32, one launch (start us, length us, event | category | flops | bytes accessed | tf_op | source)
XLA Modules:
  0.0 605.8 jit_solution(13952073995251404903)
XLA Ops:
  8.1 69.1 %all_gather.25 = bf16[192,1536]{0,1:T(8,128)(2,1)S(1)} all-gather(bf16[192,24]{0,1:T(8,128)(2,1)} %param.10), channel_id=1, replica_groups=mesh['seq'=64,'tensor'=8] {'seq'}, dimensions={1}, use_global_device_ids=true | all-gather | bytes 599040 | tf_op jit(solution)/shard_map/all_gather | solution.py:86
  80.6 5.0 collective-permute-start.4
  85.6 1.9 collective-permute-start.5
  88.9 65.4 %all_gather.31 = bf16[5,768,96]{2,0,1:T(8,128)(2,1)S(1)} all-gather(bf16[5,12,96]{2,0,1:T(8,128)(2,1)S(1)} %copy.52), channel_id=1, replica_groups=mesh['seq'=64,'tensor'=8] {'seq'}, dimensions={1}, use_global_device_ids=true | all-gather | bytes 748800 | tf_op jit(solution)/shard_map/all_gather | solution.py:88
  160.6 62.1 %all_gather.29 = bf16[1536,2,96]{2,0,1:T(8,128)(2,1)S(1)} all-gather(bf16[24,2,96]{2,0,1:T(8,128)(2,1)} %copy.46), channel_id=1, replica_groups=mesh['seq'=64,'tensor'=8] {'seq'}, dimensions={0}, use_global_device_ids=true | all-gather | bytes 599040 | tf_op jit(solution)/shard_map/all_gather | solution.py:87
  228.3 1.9 fusion.5
  231.3 37.2 %all_gather.26 = bf16[2,64,1536]{1,0,2:T(2,128)(2,1)S(1)} all-gather(bf16[2,64,192]{1,0,2:T(2,128)(2,1)S(1)} %bitcast.93), channel_id=1, replica_groups=mesh['seq'=64,'tensor'=8] {'tensor'}, dimensions={2}, use_global_device_ids=true | all-gather | bytes 442368 | tf_op jit(solution)/shard_map/all_gather | solution.py:94
  272.6 1.9 collective-permute-start
  274.5 3.6 collective-permute-start.1
  285.5 35.9 %all_gather.28 = bf16[2,64,1536]{1,0,2:T(2,128)(2,1)S(1)} all-gather(bf16[2,64,192]{1,0,2:T(2,128)(2,1)S(1)} %copy.45), channel_id=1, replica_groups=mesh['seq'=64,'tensor'=8] {'tensor'}, dimensions={2}, use_global_device_ids=true | all-gather | bytes 442368 | tf_op jit(solution)/shard_map/all_gather | solution.py:49
  322.6 34.9 %all_gather.30 = bf16[2,128,768]{1,0,2:T(2,128)(2,1)S(1)} all-gather(bf16[2,128,96]{1,0,2:T(2,128)(2,1)S(1)} %copy.50), channel_id=1, replica_groups=mesh['seq'=64,'tensor'=8] {'tensor'}, dimensions={2}, use_global_device_ids=true | all-gather | bytes 442368 | tf_op jit(solution)/shard_map/all_gather | solution.py:49
  358.8 1.9 multiply_reduce_fusion.1
  365.2 1.9 collective-permute-start.2
  367.4 1.6 copy.62
  368.9 3.6 collective-permute-start.3
  375.0 69.0 %reduce-scatter.9.cloned.1.call-done = bf16[192,128]{1,0:T(8,128)(2,1)} async-done(((bf16[1536,128]{1,0:T(8,128)(2,1)}), bf16[192,128]{1,0:T(8,128)(2,1)}) %reduce-scatter.9.cloned.1.call-update) | async-done | bytes 49168
  445.0 1.9 collective-permute-start.6
  447.0 2.6 collective-permute-start.7
  452.6 1.6 fusion.44
  454.2 1.6 fusion
  455.9 2.3 fusion.2
  459.4 99.1 %all-reduce.5.cloned.1.call-done = bf16[2,64,1536]{2,1,0:T(8,128)(2,1)} async-done(((bf16[2,64,1536]{2,1,0:T(8,128)(2,1)}), bf16[2,64,1536]{2,1,0:T(8,128)(2,1)}) %all-reduce.5.cloned.1.call-update) | async-done | bytes 393232 | tf_op jit(solution)/shard_map/psum | solution.py:70
  558.5 1.8 multiply_reduce_fusion
  561.6 36.0 %all_gather.32 = bf16[2,64,1536]{1,0,2:T(2,128)(2,1)S(1)} all-gather(bf16[2,64,192]{1,0,2:T(2,128)(2,1)S(1)} %copy.60), channel_id=1, replica_groups=mesh['seq'=64,'tensor'=8] {'tensor'}, dimensions={2}, use_global_device_ids=true | all-gather | bytes 442368 | tf_op jit(solution)/shard_map/all_gather | solution.py:49
  (123 shorter events, 46.1 us)
Async XLA Ops:
  8.0 69.1 %copy-start = (bf16[2,64,192]{2,1,0:T(8,128)(2,1)S(1)}, bf16[2,64,192]{2,1,0:T(8,128)(2,1)}, u32[]{:S(2)}) copy-start(bf16[2,64,192]{2,1,0:T(8,128)(2,1)} %param.9) | copy-start | bytes 147460
  8.0 71.9 %copy-start.1 = (bf16[2,128,96]{1,2,0:T(8,128)(2,1)S(1)}, bf16[2,128,96]{1,2,0:T(8,128)(2,1)}, u32[]{:S(2)}) copy-start(bf16[2,128,96]{1,2,0:T(8,128)(2,1)} %param.17) | copy-start | bytes 147460
  8.0 80.3 %copy-start.15 = (bf16[24,2,96]{2,1,0:T(2,128)(2,1)S(1)}, bf16[24,2,96]{2,1,0:T(2,128)(2,1)}, u32[]{:S(2)}) copy-start(bf16[24,2,96]{2,1,0:T(2,128)(2,1)} %param.13) | copy-start | bytes 27652
  8.0 80.9 %copy-start.12 = (bf16[5,12,96]{2,1,0:T(8,128)(2,1)S(1)}, bf16[5,12,96]{2,1,0:T(8,128)(2,1)}, u32[]{:S(2)}) copy-start(bf16[5,12,96]{2,1,0:T(8,128)(2,1)} %param.16) | copy-start | bytes 34564
  8.0 222.3 %reduce-scatter.7.cloned.1.call-start = ((), (), s32[]{:S(2)}) async-start(), calls=%async_computation.5 | async-start | bytes 442368
  79.3 198.9 %all-gather.2.cloned.1.call-start = ((), (), s32[]{:S(2)}) async-start(), calls=%async_computation.2 | async-start | bytes 3993600 | tf_op jit(solution)/shard_map/all_gather | solution.py:99
  79.8 278.9 %all-reduce.3.cloned.1.call-start = ((), (), s32[]{:S(2)}) async-start(), calls=%async_computation.3 | async-start | bytes 786432 | tf_op jit(solution)/shard_map/psum | solution.py:70
  80.6 142.4 %collective-permute-start.4 = (bf16[2,2,96]{1,2,0:T(8,128)(2,1)}, bf16[2,2,96]{1,2,0:T(8,128)(2,1)}, u32[]{:S(2)}, u32[]{:S(2)}) collective-permute-start(bf16[2,2,96]{1,2,0:T(8,128)(2,1)} %get-tuple-element.28), channel_id=1, source_target_pairs={{8,0},{16,8},{24,16},{32,24},{40,32},{48,40},{56,48},{64,56},{72,6... | collective-permute-start | bytes 2312 | tf_op jit(solution)/shard_map/ppermute | solution.py:19
  85.6 138.8 %collective-permute-start.5 = (bf16[2,2,96]{1,2,0:T(8,128)(2,1)}, bf16[2,2,96]{1,2,0:T(8,128)(2,1)}, u32[]{:S(2)}, u32[]{:S(2)}) collective-permute-start(bf16[2,2,96]{1,2,0:T(8,128)(2,1)} %get-tuple-element.29), channel_id=1, source_target_pairs={{0,8},{8,16},{16,24},{24,32},{32,40},{40,48},{48,56},{56,64},{64,7... | collective-permute-start | bytes 2312 | tf_op jit(solution)/shard_map/ppermute | solution.py:18
  159.7 67.3 %copy-start.4 = (bf16[1,768,96]{1,2,0:T(8,128)(2,1)S(1)}, bf16[1,768,96]{1,2,0:T(8,128)(2,1)}, u32[]{:S(2)}) copy-start(bf16[1,768,96]{1,2,0:T(8,128)(2,1)} %copy.75) | copy-start | bytes 442372
  160.4 68.0 %copy-start.2 = (bf16[1,768,96]{1,2,0:T(8,128)(2,1)S(1)}, bf16[1,768,96]{1,2,0:T(8,128)(2,1)}, u32[]{:S(2)}) copy-start(bf16[1,768,96]{1,2,0:T(8,128)(2,1)} %copy.78) | copy-start | bytes 442372
  230.3 213.7 %reduce-scatter.9.cloned.1.call-start = ((), (), s32[]{:S(2)}) async-start(), calls=%async_computation.6 | async-start | bytes 442368
  271.4 12.5 %copy-start.9 = (bf16[2,64,192]{2,1,0:T(8,128)(2,1)S(1)}, bf16[2,64,192]{2,1,0:T(8,128)(2,1)}, u32[]{:S(2)}) copy-start(bf16[2,64,192]{2,1,0:T(8,128)(2,1)} %copy.67) | copy-start | bytes 147460
  272.6 7.0 %collective-permute-start = (bf16[2,2,1536]{2,1,0:T(2,128)(2,1)S(1)}, bf16[2,2,1536]{2,1,0:T(2,128)(2,1)S(1)}, u32[]{:S(2)}, u32[]{:S(2)}) collective-permute-start(bf16[2,2,1536]{2,1,0:T(2,128)(2,1)S(1)} %get-tuple-element.24), channel_id=1, source_target_pairs={{0,8},{8,16},{16,24},{24,32},{32,40},{40,48},{48,56},{56,64},{64,7... | collective-permute-start | bytes 36872 | tf_op jit(solution)/shard_map/ppermute | solution.py:18
  274.5 6.5 %collective-permute-start.1 = (bf16[2,2,1536]{2,1,0:T(2,128)(2,1)S(1)}, bf16[2,2,1536]{2,1,0:T(2,128)(2,1)S(1)}, u32[]{:S(2)}, u32[]{:S(2)}) collective-permute-start(bf16[2,2,1536]{2,1,0:T(2,128)(2,1)S(1)} %get-tuple-element.25), channel_id=1, source_target_pairs={{8,0},{16,8},{24,16},{32,24},{40,32},{48,40},{56,48},{64,56},{72,6... | collective-permute-start | bytes 36872 | tf_op jit(solution)/shard_map/ppermute | solution.py:19
  282.5 39.5 %copy-start.10 = (bf16[2,128,96]{1,2,0:T(8,128)(2,1)S(1)}, bf16[2,128,96]{1,2,0:T(8,128)(2,1)}, u32[]{:S(2)}) copy-start(bf16[2,128,96]{1,2,0:T(8,128)(2,1)} %param.14) | copy-start | bytes 147460
  365.1 193.4 %all-reduce.5.cloned.1.call-start = ((), (), s32[]{:S(2)}) async-start(), calls=%async_computation.4 | async-start | bytes 786432 | tf_op jit(solution)/shard_map/psum | solution.py:70
  365.2 7.4 %collective-permute-start.2 = (bf16[2,2,768]{2,1,0:T(2,128)(2,1)S(1)}, bf16[2,2,768]{2,1,0:T(2,128)(2,1)S(1)}, u32[]{:S(2)}, u32[]{:S(2)}) collective-permute-start(bf16[2,2,768]{2,1,0:T(2,128)(2,1)S(1)} %get-tuple-element.22), channel_id=1, source_target_pairs={{0,8},{8,16},{16,24},{24,32},{32,40},{40,48},{48,56},{56,64},{64,7... | collective-permute-start | bytes 18440 | tf_op jit(solution)/shard_map/ppermute | solution.py:18
  368.9 89.3 %collective-permute-start.3 = (bf16[2,2,768]{2,1,0:T(2,128)(2,1)S(1)}, bf16[2,2,768]{2,1,0:T(2,128)(2,1)S(1)}, u32[]{:S(2)}, u32[]{:S(2)}) collective-permute-start(bf16[2,2,768]{2,1,0:T(2,128)(2,1)S(1)} %get-tuple-element.23), channel_id=1, source_target_pairs={{8,0},{16,8},{24,16},{32,24},{40,32},{48,40},{56,48},{64,56},{72,6... | collective-permute-start | bytes 18440 | tf_op jit(solution)/shard_map/ppermute | solution.py:19
  445.0 6.1 collective-permute-start.6
  447.0 5.7 collective-permute-start.7
  454.2 104.3 %copy-start.11 = (f32[1536]{0:T(1024)S(1)}, f32[1536]{0:T(1024)}, u32[]{:S(2)}) copy-start(f32[1536]{0:T(1024)} %param.11) | copy-start | bytes 18436
  454.2 104.3 %copy-start.14 = (f32[2,64]{1,0:T(2,128)S(1)}, f32[2,64]{1,0:T(2,128)}, u32[]{:S(2)}) copy-start(f32[2,64]{1,0:T(2,128)} %copy-done.13) | copy-start | bytes 1540
  455.8 104.5 %copy-start.17 = (f32[2,64]{1,0:T(2,128)S(1)}, f32[2,64]{1,0:T(2,128)}, u32[]{:S(2)}) copy-start(f32[2,64]{1,0:T(2,128)} %copy-done.16) | copy-start | bytes 1540
  (8 other events, 21.1 us)
Sparse Core Ops, SparseCore 0:
  79.4 80.6 reduce-scatter.6
  230.4 92.9 all-reduce.2
  365.2 78.7 reduce-scatter.8
  458.3 100.1 all-reduce.4
Sparse Core Ops, SparseCore 1:
  81.8 117.8 all-gather.1
where the time goes:
time: 607 us; the launch traced here: 606 us
  blocking collectives  341 us (56%)
  waiting for transfers between devices  169 us (28%)
  matrix products  27.6 us (5%)
  starting transfers between devices  22.8 us (4%)
  local copies, waits for them, and re-layouts  20.7 us (3%)
  between operations  15.9 us (3%)
  other arithmetic  9.67 us (2%)
    all_gather x3, blocking collectives, spread(): return lax.all_gather(field, 'tensor', axis=2, tiled=True)  107 us
    psum x2, waiting for transfers between devices, norm_back(): lax.psum(partial_grad.astype(jnp.bfloat16), 'tensor').astype(jnp.float32)  99.1 us
    unnamed x7, waiting for transfers between devices  69.6 us
    all_gather x1, blocking collectives, per_device(): lax.all_gather(w_out, 'seq', axis=1, tiled=True)  69.1 us
    all_gather x1, blocking collectives, per_device(): lax.all_gather(w_conv2, 'seq', axis=1, tiled=True)  65.4 us
    all_gather x1, blocking collectives, per_device(): lax.all_gather(w_up, 'seq', axis=0, tiled=True)  62.1 us
    all_gather x1, blocking collectives, per_device(): projected_full = lax.all_gather(projected, 'tensor', axis=2, tiled=True)  37.2 us
    dot_general x12, matrix products, matmul_back(): lax.dot_general(left, right, (((left.ndim - 1,), (right.ndim - 1,)), ((),...  15.9 us
  transfers between devices with their start and end apart: 13, of which 2 were waited for; matrix products, arithmetic and copies ran while one was open for 7% of the time, Pallas kernels for 0%

commit v1 on v0

--- a/solution.py
+++ b/solution.py
@@ -1,3 +1,4 @@
+import functools
 import jax
 import jax.numpy as jnp
 from jax import lax
@@ -6,6 +7,21 @@
 C_COARSE = 1536
 C_FINE = 768
 EPS = 1e-06
+
+
+def pass_cube(base_x, lane_axis):
+    return jnp.concatenate(
+        lax.all_to_all(
+            jnp.stack([base_x] * lax.axis_size(lane_axis), axis=0),
+            axis_name=lane_axis,
+            concat_axis=0,
+            split_axis=0,
+        ),
+        2,
+    )
+
+
+classes_search = functools.partial(pass_cube, lane_axis="tensor")
 
 
 def extended(shard, sides, width):
@@ -46,7 +62,7 @@
 
 
 def spread(field):
-    return lax.all_gather(field, "tensor", axis=2, tiled=True)
+    return classes_search(field)
 
 
 def conv_rows(total, wide, piece):

time: 607 us -> 631 us (1.040)
  waiting for transfers between devices: 169 us -> 289 us
  blocking collectives: 341 us -> 232 us
  starting transfers between devices: 22.8 us -> 36.4 us
    all_gather x3 -> x0, blocking collectives: 107 us -> none  [spread(): return lax.all_gather(field, 'tensor', axis=2, tiled=True)]
    psum x2, waiting for transfers between devices: 99.1 us -> 188 us  [norm_back(): lax.psum(partial_grad.astype(jnp.bfloat16), 'tensor').astype(jnp.float32)]
    all_to_all x0 -> x3, waiting for transfers between devices: none -> 21.9 us  [pass_cube(): lax.all_to_all(jnp.stack([base_x] * lax.axis_size(lane_axis), axis=0), ax...]
    all_to_all x0 -> x3, starting transfers between devices: none -> 13.6 us  [pass_cube(): lax.all_to_all(jnp.stack([base_x] * lax.axis_size(lane_axis), axis=0), ax...]
    unnamed x7, waiting for transfers between devices: 69.6 us -> 78.4 us
    unnamed x56 -> x60, local copies, waits for them, and re-layouts: 15.2 us -> 11.7 us
  transfers between devices with their start and end apart: 13 -> 16, of which waited for: 2 -> 6; matrix products, arithmetic and copies ran while one was open for 7% -> 7% of each run, Pallas kernels for 0% -> 0%
where the time goes in v1:
time: 631 us; the launch traced here: 630 us
  waiting for transfers between devices  289 us (46%)
  blocking collectives  232 us (37%)
  starting transfers between devices  36.4 us (6%)
  matrix products  27.9 us (4%)
  local copies, waits for them, and re-layouts  22 us (3%)
  between operations  15.9 us (3%)
  other arithmetic  6.83 us (1%)
    psum x2, waiting for transfers between devices, norm_back(): lax.psum(partial_grad.astype(jnp.bfloat16), 'tensor').astype(jnp.float32)  188 us
    unnamed x7, waiting for transfers between devices  78.4 us
    all_gather x1, blocking collectives, per_device(): lax.all_gather(w_out, 'seq', axis=1, tiled=True)  69.1 us
    all_gather x1, blocking collectives, per_device(): lax.all_gather(w_conv2, 'seq', axis=1, tiled=True)  65 us
    all_gather x1, blocking collectives, per_device(): lax.all_gather(w_up, 'seq', axis=0, tiled=True)  62.1 us
    all_gather x1, blocking collectives, per_device(): projected_full = lax.all_gather(projected, 'tensor', axis=2, tiled=True)  35.5 us
    all_to_all x3, waiting for transfers between devices, pass_cube(): lax.all_to_all(jnp.stack([base_x] * lax.axis_size(lane_axis), axis=0), ax...  21.9 us
    dot_general x12, matrix products, matmul_back(): lax.dot_general(left, right, (((left.ndim - 1,), (right.ndim - 1,)), ((),...  17.2 us
  transfers between devices with their start and end apart: 16, of which 6 were waited for; matrix products, arithmetic and copies ran while one was open for 7% of the time, Pallas kernels for 0%

profile of v1, /device:TPU:32, one launch (start us, length us, event | category | flops | bytes accessed | tf_op | source)
XLA Modules:
  0.0 629.5 jit_solution(4065376275041626075)
XLA Ops:
  8.1 69.1 %all_gather.16 = bf16[192,1536]{0,1:T(8,128)(2,1)S(1)} all-gather(bf16[192,24]{0,1:T(8,128)(2,1)} %param.10), channel_id=1, replica_groups=mesh['seq'=64,'tensor'=8] {'seq'}, dimensions={1}, use_global_device_ids=true | all-gather | bytes 599040 | tf_op jit(solution)/shard_map/all_gather | solution.py:102
  80.6 5.0 collective-permute-start.4
  85.6 1.9 collective-permute-start.5
  88.3 65.0 %all_gather.20 = bf16[5,768,96]{2,0,1:T(8,128)(2,1)S(1)} all-gather(bf16[5,12,96]{2,0,1:T(8,128)(2,1)S(1)} %copy.43), channel_id=1, replica_groups=mesh['seq'=64,'tensor'=8] {'seq'}, dimensions={1}, use_global_device_ids=true | all-gather | bytes 748800 | tf_op jit(solution)/shard_map/all_gather | solution.py:104
  158.2 62.1 %all_gather.19 = bf16[1536,2,96]{2,0,1:T(8,128)(2,1)S(1)} all-gather(bf16[24,2,96]{2,0,1:T(8,128)(2,1)S(1)} %copy.38), channel_id=1, replica_groups=mesh['seq'=64,'tensor'=8] {'seq'}, dimensions={0}, use_global_device_ids=true | all-gather | bytes 599040 | tf_op jit(solution)/shard_map/all_gather | solution.py:103
  224.3 35.5 %all_gather.17 = bf16[2,64,1536]{1,0,2:T(2,128)(2,1)S(1)} all-gather(bf16[2,64,192]{1,0,2:T(2,128)(2,1)S(1)} %bitcast.112), channel_id=1, replica_groups=mesh['seq'=64,'tensor'=8] {'tensor'}, dimensions={2}, use_global_device_ids=true | all-gather | bytes 442368 | tf_op jit(solution)/shard_map/all_gather | solution.py:110
  261.0 1.9 collective-permute-start
  262.9 3.6 collective-permute-start.1
  274.6 6.7 %all-to-all-start = ((bf16[8,2,64,192]{3,2,1,0:T(8,128)(2,1)}), bf16[8,2,64,192]{3,2,1,0:T(8,128)(2,1)S(1)}, u32[]{:S(2)}, u32[]{:S(2)}) async-start(bf16[8,2,64,192]{3,2,1,0:T(8,128)(2,1)} %stack.6), calls=%async_computation | async-start | bytes 1048576 | tf_op jit(solution)/shard_map/all_to_all | solution.py:14
  283.3 8.1 %all-to-all-done = bf16[8,2,64,192]{3,2,1,0:T(8,128)(2,1)S(1)} async-done(((bf16[8,2,64,192]{3,2,1,0:T(8,128)(2,1)}), bf16[8,2,64,192]{3,2,1,0:T(8,128)(2,1)S(1)}, u32[]{:S(2)}, u32[]{:S(2)}) %all-to-all-start) | async-done | bytes 393248 | tf_op jit(solution)/shard_map/all_to_all | solution.py:14
  297.9 3.5 all-to-all-start.1
  302.7 2.0 fusion.5
  304.8 5.4 all-to-all-done.1
  310.7 88.4 %all-reduce.3.cloned.1.call-done = bf16[2,128,768]{2,1,0:T(8,128)(2,1)} async-done(((bf16[2,128,768]{2,1,0:T(8,128)(2,1)}), bf16[2,128,768]{2,1,0:T(8,128)(2,1)}) %all-reduce.3.cloned.1.call-update) | async-done | bytes 393232 | tf_op jit(solution)/shard_map/psum | solution.py:86
  399.2 2.5 multiply_reduce_fusion.1
  406.1 1.9 collective-permute-start.2
  408.0 3.8 collective-permute-start.3
  412.4 77.8 %reduce-scatter.9.cloned.1.call-done = bf16[192,128]{1,0:T(8,128)(2,1)} async-done(((bf16[1536,128]{1,0:T(8,128)(2,1)}), bf16[192,128]{1,0:T(8,128)(2,1)}) %reduce-scatter.9.cloned.1.call-update) | async-done | bytes 49168
  491.2 1.9 collective-permute-start.6
  493.2 2.4 collective-permute-start.7
  501.8 2.3 fusion.2
  504.8 100.0 %all-reduce.5.cloned.1.call-done = bf16[2,64,1536]{2,1,0:T(8,128)(2,1)} async-done(((bf16[2,64,1536]{2,1,0:T(8,128)(2,1)}), bf16[2,64,1536]{2,1,0:T(8,128)(2,1)}) %all-reduce.5.cloned.1.call-update) | async-done | bytes 393232 | tf_op jit(solution)/shard_map/psum | solution.py:86
  607.7 3.5 all-to-all-start.2
  612.4 8.4 %all-to-all-done.2 = bf16[8,2,64,192]{3,2,1,0:T(8,128)(2,1)S(1)} async-done(((bf16[8,2,64,192]{3,2,1,0:T(8,128)(2,1)}), bf16[8,2,64,192]{3,2,1,0:T(8,128)(2,1)S(1)}, u32[]{:S(2)}, u32[]{:S(2)}) %all-to-all-start.2) | async-done | bytes 393248 | tf_op jit(solution)/shard_map/all_to_all | solution.py:14
  (136 shorter events, 50.7 us)
Async XLA Ops:
  8.0 80.2 %copy-start.18 = (bf16[24,2,96]{2,1,0:T(2,128)(2,1)S(1)}, bf16[24,2,96]{2,1,0:T(2,128)(2,1)}, u32[]{:S(2)}) copy-start(bf16[24,2,96]{2,1,0:T(2,128)(2,1)} %param.13) | copy-start | bytes 27652
  8.0 215.2 %reduce-scatter.7.cloned.1.call-start = ((), (), s32[]{:S(2)}) async-start(), calls=%async_computation.8 | async-start | bytes 442368
  79.3 187.3 %all-gather.2.cloned.1.call-start = ((), (), s32[]{:S(2)}) async-start(), calls=%async_computation.5 | async-start | bytes 3993600 | tf_op jit(solution)/shard_map/all_gather | solution.py:115
  80.6 142.7 %collective-permute-start.4 = (bf16[2,2,96]{1,2,0:T(8,128)(2,1)S(1)}, bf16[2,2,96]{1,2,0:T(8,128)(2,1)S(1)}, u32[]{:S(2)}, u32[]{:S(2)}) collective-permute-start(bf16[2,2,96]{1,2,0:T(8,128)(2,1)S(1)} %get-tuple-element.28), channel_id=1, source_target_pairs={{8,0},{16,8},{24,16},{32,24},{40,32},{48,40},{56,48},{64,56},{72,6... | collective-permute-start | bytes 2312 | tf_op jit(solution)/shard_map/ppermute | solution.py:35
  85.6 215.8 %collective-permute-start.5 = (bf16[2,2,96]{1,2,0:T(8,128)(2,1)}, bf16[2,2,96]{1,2,0:T(8,128)(2,1)}, u32[]{:S(2)}, u32[]{:S(2)}) collective-permute-start(bf16[2,2,96]{1,2,0:T(8,128)(2,1)} %get-tuple-element.29), channel_id=1, source_target_pairs={{0,8},{8,16},{16,24},{24,32},{32,40},{40,48},{48,56},{56,64},{64,7... | collective-permute-start | bytes 2312 | tf_op jit(solution)/shard_map/ppermute | solution.py:34
  156.0 104.5 %copy-start.15 = (f32[1536]{0:T(1024)S(1)}, f32[1536]{0:T(1024)}, u32[]{:S(2)}) copy-start(f32[1536]{0:T(1024)} %param.11) | copy-start | bytes 18436
  261.0 7.0 %collective-permute-start = (bf16[2,2,1536]{2,1,0:T(2,128)(2,1)S(1)}, bf16[2,2,1536]{2,1,0:T(2,128)(2,1)S(1)}, u32[]{:S(2)}, u32[]{:S(2)}) collective-permute-start(bf16[2,2,1536]{2,1,0:T(2,128)(2,1)S(1)} %get-tuple-element.24), channel_id=1, source_target_pairs={{0,8},{8,16},{16,24},{24,32},{32,40},{40,48},{48,56},{56,64},{64,7... | collective-permute-start | bytes 36872 | tf_op jit(solution)/shard_map/ppermute | solution.py:34
  262.9 6.5 %collective-permute-start.1 = (bf16[2,2,1536]{2,1,0:T(2,128)(2,1)S(1)}, bf16[2,2,1536]{2,1,0:T(2,128)(2,1)S(1)}, u32[]{:S(2)}, u32[]{:S(2)}) collective-permute-start(bf16[2,2,1536]{2,1,0:T(2,128)(2,1)S(1)} %get-tuple-element.25), channel_id=1, source_target_pairs={{8,0},{16,8},{24,16},{32,24},{40,32},{48,40},{56,48},{64,56},{72,6... | collective-permute-start | bytes 36872 | tf_op jit(solution)/shard_map/ppermute | solution.py:35
  274.6 16.8 %all-to-all-start = ((bf16[8,2,64,192]{3,2,1,0:T(8,128)(2,1)}), bf16[8,2,64,192]{3,2,1,0:T(8,128)(2,1)S(1)}, u32[]{:S(2)}, u32[]{:S(2)}) async-start(bf16[8,2,64,192]{3,2,1,0:T(8,128)(2,1)} %stack.6), calls=%async_computation | async-start | bytes 1048576 | tf_op jit(solution)/shard_map/all_to_all | solution.py:14
  297.0 102.1 %copy-start.17 = (f32[768]{0:T(1024)S(1)}, f32[768]{0:T(1024)}, u32[]{:S(2)}) copy-start(f32[768]{0:T(1024)} %param.15) | copy-start | bytes 9220
  297.9 12.4 %all-to-all-start.1 = ((bf16[8,2,128,96]{2,3,1,0:T(8,128)(2,1)}), bf16[8,2,128,96]{2,3,1,0:T(8,128)(2,1)S(1)}, u32[]{:S(2)}, u32[]{:S(2)}) async-start(bf16[8,2,128,96]{2,3,1,0:T(8,128)(2,1)} %stack.7), calls=%async_computation.1 | async-start | bytes 786432 | tf_op jit(solution)/shard_map/all_to_all | solution.py:14
  301.3 97.8 %all-reduce.3.cloned.1.call-start = ((), (), s32[]{:S(2)}) async-start(), calls=%async_computation.6 | async-start | bytes 786432 | tf_op jit(solution)/shard_map/psum | solution.py:86
  302.7 99.0 %copy-start.10 = (bf16[2,128,96]{2,1,0:T(8,128)(2,1)S(1)}, bf16[2,128,96]{2,1,0:T(8,128)(2,1)}, u32[]{:S(2)}) copy-start(bf16[2,128,96]{2,1,0:T(8,128)(2,1)} %copy.50) | copy-start | bytes 147460
  304.7 185.5 %reduce-scatter.9.cloned.1.call-start = ((), (), s32[]{:S(2)}) async-start(), calls=%async_computation.9 | async-start | bytes 442368
  405.1 199.7 %all-reduce.5.cloned.1.call-start = ((), (), s32[]{:S(2)}) async-start(), calls=%async_computation.7 | async-start | bytes 786432 | tf_op jit(solution)/shard_map/psum | solution.py:86
  406.1 98.1 %collective-permute-start.2 = (bf16[2,2,768]{2,1,0:T(2,128)(2,1)S(1)}, bf16[2,2,768]{2,1,0:T(2,128)(2,1)S(1)}, u32[]{:S(2)}, u32[]{:S(2)}) collective-permute-start(bf16[2,2,768]{2,1,0:T(2,128)(2,1)S(1)} %get-tuple-element.22), channel_id=1, source_target_pairs={{0,8},{8,16},{16,24},{24,32},{32,40},{40,48},{48,56},{56,64},{64,7... | collective-permute-start | bytes 18440 | tf_op jit(solution)/shard_map/ppermute | solution.py:34
  408.0 203.2 %collective-permute-start.3 = (bf16[2,2,768]{2,1,0:T(2,128)(2,1)S(1)}, bf16[2,2,768]{2,1,0:T(2,128)(2,1)S(1)}, u32[]{:S(2)}, u32[]{:S(2)}) collective-permute-start(bf16[2,2,768]{2,1,0:T(2,128)(2,1)S(1)} %get-tuple-element.23), channel_id=1, source_target_pairs={{8,0},{16,8},{24,16},{32,24},{40,32},{48,40},{56,48},{64,56},{72,6... | collective-permute-start | bytes 18440 | tf_op jit(solution)/shard_map/ppermute | solution.py:35
  491.2 5.9 collective-permute-start.6
  493.2 5.5 collective-permute-start.7
  501.8 104.8 %copy-start.20 = (f32[2,64]{1,0:T(2,128)S(1)}, f32[2,64]{1,0:T(2,128)}, u32[]{:S(2)}) copy-start(f32[2,64]{1,0:T(2,128)} %copy-done.19) | copy-start | bytes 1540
  501.8 109.4 %copy-start.6 = (bf16[1,768,96]{1,2,0:T(8,128)(2,1)S(1)}, bf16[1,768,96]{1,2,0:T(8,128)(2,1)}, u32[]{:S(2)}) copy-start(bf16[1,768,96]{1,2,0:T(8,128)(2,1)} %copy.71) | copy-start | bytes 442372
  504.2 107.3 %copy-start.4 = (bf16[1,768,96]{1,2,0:T(8,128)(2,1)S(1)}, bf16[1,768,96]{1,2,0:T(8,128)(2,1)}, u32[]{:S(2)}) copy-start(bf16[1,768,96]{1,2,0:T(8,128)(2,1)} %copy.70) | copy-start | bytes 442372
  504.2 107.3 %copy-start.14 = (bf16[2,128,96]{1,2,0:T(8,128)(2,1)S(1)}, bf16[2,128,96]{1,2,0:T(8,128)(2,1)}, u32[]{:S(2)}) copy-start(bf16[2,128,96]{1,2,0:T(8,128)(2,1)} %copy-done.13) | copy-start | bytes 147460
  607.7 13.1 %all-to-all-start.2 = ((bf16[8,2,64,192]{3,2,1,0:T(8,128)(2,1)}), bf16[8,2,64,192]{3,2,1,0:T(8,128)(2,1)S(1)}, u32[]{:S(2)}, u32[]{:S(2)}) async-start(bf16[8,2,64,192]{3,2,1,0:T(8,128)(2,1)} %stack.8), calls=%async_computation.2 | async-start | bytes 1048576 | tf_op jit(solution)/shard_map/all_to_all | solution.py:14
  (13 other events, 288.1 us)
Sparse Core Ops, SparseCore 0:
  79.4 80.6 reduce-scatter.6
  305.1 94.0 all-reduce.2
  405.3 84.9 reduce-scatter.8
  504.3 100.4 all-reduce.4
Sparse Core Ops, SparseCore 1:
  81.8 117.9 all-gather.1
